TPU v7x, 128 devices: a whole 4x4x4 slice. The times are simulated.
128 devices in a mesh: gr: 16 (over x, y), gc: 8 (over z, core).
Axes of the slice: x: 4, y: 4, z: 4, core: 2. Of those that a mesh axis runs over, the one named last changes fastest.
Arguments:
- child_rows: float32 [8192, 12288], P('gr', 'gc'), may hold values from -1.5 to 1.5
- row_map: int32 [8192], P('gr'), may hold values from 0 to 8191, as said below
- stair: int32 [64], replicated, may hold values from 0 to 896, as said below
Outputs:
- factor: float32 [1024, 12288], P('gr', 'gc')
- projected: float32 [8192, 12288], P('gr', 'gc')
Inputs may be any that keep to these rules, and one draw needn't show every extreme that they name: row_map is a permutation of 0 to 8191. Of the 512 rows of one index of gr, at most 152 go to the rows of any one index of gr (row_map // 512), and some index of gr sends exactly 152 to one index. stair is nondecreasing and a multiple of 128; the first quarter of the blocks is 0 and the last block holds 896.
All inputs are finite; a program needn't handle non-finite values.
Results may differ from a plain program's by a relative error of at most 0.0003.
Values sent between devices are 32-bit elements; how exact they have to be, the bound alone decides.
A program may use at most 128 MiB of HBM per device.

v0:
```python
import jax
import jax.numpy as jnp
from jax import lax
from jax.sharding import PartitionSpec as P

PANEL = 512
NPANEL = 2
STAIR_BLOCK = 128


def spread(value, axis, source):
    kept = jnp.where(lax.axis_index(axis) == source, value, 0).astype(value.dtype)
    return lax.psum(kept, axis)


def pack_rows(values, targets, groups):
    rows_dev = values.shape[0]
    base_rows = 3 * rows_dev // (4 * groups)
    capacity = rows_dev - base_rows * (groups - 1)
    target_dev = targets // rows_dev
    target_row = targets % rows_dev
    onehot = (target_dev[:, None] == jnp.arange(groups, dtype=jnp.int32)[None, :]).astype(jnp.int32)
    rank_within = jnp.sum((jnp.cumsum(onehot, axis=0) - onehot) * onehot, axis=1)
    buffer_index = target_dev * capacity + rank_within
    source_row = (
        jnp.full((groups * capacity,), rows_dev, jnp.int32)
        .at[buffer_index]
        .set(jnp.arange(rows_dev, dtype=jnp.int32))
    )
    sent_rows = jnp.take(values, source_row, axis=0, mode="fill", fill_value=0.0)
    sent_slots = (
        jnp.full((groups * capacity,), rows_dev, jnp.int32).at[buffer_index].set(target_row)
    )
    return (
        sent_rows.reshape(groups, capacity, values.shape[1]),
        sent_slots.reshape(groups, capacity),
    )


def place_rows(recv_rows, recv_slots, rows_dev):
    flat_rows = recv_rows.reshape(-1, recv_rows.shape[-1])
    flat_slots = recv_slots.reshape(-1)
    where_from = (
        jnp.zeros((rows_dev,), jnp.int32)
        .at[flat_slots]
        .set(jnp.arange(flat_slots.shape[0], dtype=jnp.int32), mode="drop")
    )
    return jnp.take(flat_rows, where_from, axis=0)


def matmul(left, right):
    return jnp.dot(left, right, precision=lax.Precision.HIGHEST, preferred_element_type=jnp.float32)


def shards(child_rows, row_map, stair):
    groups = lax.axis_size("gr")
    rows_dev, cols_dev = child_rows.shape
    columns = lax.axis_index("gc") * cols_dev + jnp.arange(cols_dev, dtype=jnp.int32)
    sent_rows, sent_slots = pack_rows(child_rows, row_map, groups)
    recv_rows, recv_slots = (
        lax.all_to_all(sent_rows, "gr", split_axis=0, concat_axis=0, tiled=True),
        lax.all_to_all(sent_slots, "gr", split_axis=0, concat_axis=0, tiled=True),
    )
    front_work = place_rows(recv_rows, recv_slots, rows_dev)
    own_rows = lax.axis_index("gr") * rows_dev + jnp.arange(rows_dev, dtype=jnp.int32)
    limits = jnp.take(stair, own_rows // STAIR_BLOCK)
    front_work = jnp.where(
        columns[None, :] >= limits[:, None], front_work, jnp.zeros_like(front_work)
    )
    blocks = []
    for step in range(NPANEL):
        panel_block = spread(front_work[:, step * PANEL : (step + 1) * PANEL], "gc", 0)
        gram_one = lax.psum(matmul(panel_block.T, panel_block), "gr")
        lower_one = jnp.linalg.cholesky(gram_one)
        basis_cols = jax.scipy.linalg.solve_triangular(lower_one, panel_block.T, lower=True).T
        coupling = lax.psum(matmul(basis_cols.T, front_work), "gr")
        front_work = front_work - matmul(basis_cols, coupling)
        blocks.append(coupling)
    stacked = jnp.concatenate(blocks, axis=0)
    share_rows = stacked.shape[0] // groups
    factor = lax.dynamic_slice_in_dim(stacked, lax.axis_index("gr") * share_rows, share_rows, 0)
    return (factor, front_work)


def solution(mesh):
    placed = (P("gr", "gc"), P("gr"), P())
    return jax.shard_map(
        shards,
        mesh=mesh,
        in_specs=placed,
        out_specs=(P("gr", "gc"), P("gr", "gc")),
        check_vma=False,
    )
```

profile of v0, /device:TPU:1, one launch (start us, length us, event | category | flops | bytes accessed | tf_op | source)
XLA Modules:
  0.0 1196.0 jit_solution(4208776243515195790)
XLA Ops:
  9.6 2.5 scatter_custom_fusion
  12.7 7.6 all-to-all-start
  20.3 2.5 scatter_custom_fusion.2
  23.0 10.1 gather_fusion
  33.1 11.6 broadcast_select_fusion
  44.7 6.8 all-to-all-start.1
  54.2 4.4 compare_select_fusion.3
  60.1 35.7 %select_select_fusion.3 = s32[512]{0:T(512)S(1)} fusion(pred[512]{0:T(512)(128)(4,1)S(1)} %get-tuple-element.130, pred[512]{0:T(512)(128)(4,1)S(1)} %get-tuple-element.131, pred[512]{0:T(512)(128)(4,1)S(1)} %get-tuple-element.132, pred[512]{0:T(512)(128)(4,1)S(1)} %get-tuple-element.133, pred[512]{0:T(512)(128)(4,1)S(1)} %get-tuple-element.134, ...), kind=kLoop, calls=%fused_computation.224 | loop fusion | flops 40960 | bytes 33512 | tf_op jit(solution)/shard_map/jit(_take)/select_n | solution.py:66
  96.0 12.3 %scatter_custom_fusion.1 = s32[512]{0:T(512)S(1)} fusion(s32[2432]{0:T(1024)S(1)} %fusion.63, s32[2432]{0:T(1024)S(1)} %iota.86, s32[]{:T(128)} %constant.193.clone.1), kind=kCustom, calls=%fused_computation.249 | custom fusion | bytes 2052 | tf_op jit(solution)/shard_map/scatter | solution.py:46
  108.4 204.8 %all-to-all-done.1 = f32[16,152,1536]{2,1,0:T(8,128)} async-done(((f32[16,152,1536]{2,1,0:T(8,128)}), f32[16,152,1536]{2,1,0:T(8,128)}, u32[]{:S(2)}, u32[]{:S(2)}) %all-to-all-start.1) | async-done | bytes 14942240 | tf_op jit(solution)/shard_map/all_to_all | solution.py:61
  313.2 9.8 gather_fusion.1
  323.0 2.3 select_select_fusion
  326.5 69.1 %all-reduce.8.cloned.1.call-done = f32[512,512]{1,0:T(8,128)} async-done(((f32[512,512]{1,0:T(8,128)}), f32[512,512]{1,0:T(8,128)}) %all-reduce.8.cloned.1.call-update) | async-done | bytes 1048592 | tf_op jit(solution)/shard_map/psum | solution.py:13
  395.6 4.4 fusion.88
  400.5 86.2 %all-reduce.10.cloned.1.call-done = f32[512,512]{0,1:T(8,128)} async-done(((f32[512,512]{0,1:T(8,128)}), f32[512,512]{0,1:T(8,128)}) %all-reduce.10.cloned.1.call-update) | async-done | bytes 1048592 | tf_op jit(solution)/shard_map/psum | solution.py:73
  486.7 2.5 copy.11
  492.0 11.7 cholesky.286
  504.9 9.8 custom-call.27
  517.9 11.7 cholesky.305
  530.3 10.0 custom-call.28
  542.6 11.7 cholesky.326
  554.9 9.8 custom-call.29
  567.0 11.7 cholesky.343
  584.6 2.7 select_select_fusion.2
  587.3 11.7 while.4
  599.0 39.9 %custom-call.30 = f32[4,128,128]{1,2,0:T(8,128)} custom-call(f32[4,128,128]{2,1,0:T(8,128)S(1)} %get-tuple-element.18), custom_call_target="InvertDiagBlocksLowerTriangular" | custom-call | tf_op jit(solution)/shard_map/jit(_solve_triangular)/triangular_solve | solution.py:75
  645.9 2.6 convolution_subtract_fusion.7
  649.7 6.9 fusion.13
  656.6 96.0 %all-reduce.12.cloned.1.call-done = f32[512,1536]{1,0:T(8,128)} async-done(((f32[512,1536]{1,0:T(8,128)}), f32[512,1536]{1,0:T(8,128)}) %all-reduce.12.cloned.1.call-update) | async-done | bytes 3145744 | tf_op jit(solution)/shard_map/psum | solution.py:76
  752.6 7.8 convolution_subtract_fusion.1
  761.7 60.2 %all-reduce.14.cloned.1.call-done = f32[512,512]{1,0:T(8,128)} async-done(((f32[512,512]{1,0:T(8,128)}), f32[512,512]{1,0:T(8,128)}) %all-reduce.14.cloned.1.call-update) | async-done | bytes 1048592 | tf_op jit(solution)/shard_map/psum | solution.py:13
  821.9 4.5 fusion.89
  826.7 86.5 %all-reduce.16.cloned.1.call-done = f32[512,512]{0,1:T(8,128)} async-done(((f32[512,512]{0,1:T(8,128)}), f32[512,512]{0,1:T(8,128)}) %all-reduce.16.cloned.1.call-update) | async-done | bytes 1048592 | tf_op jit(solution)/shard_map/psum | solution.py:73
  913.1 2.5 copy.13
  918.4 11.7 cholesky.358
  931.3 9.8 custom-call.31
  944.3 11.7 cholesky.377
  956.6 10.0 custom-call.32
  969.0 11.7 cholesky.398
  981.3 9.8 custom-call.33
  993.4 11.7 cholesky.415
  1011.0 2.7 select_select_fusion.1
  1013.8 11.8 while.5
  1025.5 39.9 %custom-call.34 = f32[4,128,128]{1,2,0:T(8,128)} custom-call(f32[4,128,128]{2,1,0:T(8,128)S(1)} %get-tuple-element.19), custom_call_target="InvertDiagBlocksLowerTriangular" | custom-call | tf_op jit(solution)/shard_map/jit(_solve_triangular)/triangular_solve | solution.py:75
  1072.4 2.6 convolution_subtract_fusion.6
  1076.2 6.9 fusion.12
  1083.1 95.9 %all-reduce.18.cloned.1.call-done = f32[512,1536]{1,0:T(8,128)} async-done(((f32[512,1536]{1,0:T(8,128)}), f32[512,1536]{1,0:T(8,128)}) %all-reduce.18.cloned.1.call-update) | async-done | bytes 3145744 | tf_op jit(solution)/shard_map/psum | solution.py:76
  1179.0 9.2 convolution_subtract_fusion
  (183 shorter events, 83.5 us)
Async XLA Ops:
  7.2 15.8 %copy-start = (f32[512,1536]{1,0:T(8,128)S(1)}, f32[512,1536]{1,0:T(8,128)}, u32[]{:S(2)}) copy-start(f32[512,1536]{1,0:T(8,128)} %param.6) | copy-start | bytes 9437188
  12.7 32.0 %all-to-all-start = ((s32[16,1,152]{2,1,0:T(1,128)}), s32[16,1,152]{2,1,0:T(1,128)S(1)}, u32[]{:S(2)}, u32[]{:S(2)}) async-start(s32[16,1,152]{2,1,0:T(1,128)} %all_to_all.9), calls=%async_computation | async-start | bytes 32768 | tf_op jit(solution)/shard_map/all_to_all | solution.py:62
  44.7 8.1 copy-start.14
  44.7 268.5 %all-to-all-start.1 = ((f32[16,152,1536]{2,1,0:T(8,128)}), f32[16,152,1536]{2,1,0:T(8,128)}, u32[]{:S(2)}, u32[]{:S(2)}) async-start(f32[16,152,1536]{2,1,0:T(8,128)} %broadcast_select_fusion), calls=%async_computation.1 | async-start | bytes 29884416 | tf_op jit(solution)/shard_map/all_to_all | solution.py:61
  51.5 344.0 %all-reduce.8.cloned.1.call-start = ((), (), s32[]{:S(2)}) async-start(), calls=%async_computation.2 | async-start | bytes 2097152 | tf_op jit(solution)/shard_map/psum | solution.py:13
  325.3 323.6 %copy-start.3 = (f32[512,1536]{1,0:T(8,128)}, f32[512,1536]{1,0:T(8,128)S(1)}, u32[]{:S(2)}) copy-start(f32[512,1536]{1,0:T(8,128)S(1)} %select_select_fusion) | copy-start | bytes 9437188
  326.5 160.2 %all-reduce.10.cloned.1.call-start = ((), (), s32[]{:S(2)}) async-start(), calls=%async_computation.3 | async-start | bytes 2097152 | tf_op jit(solution)/shard_map/psum | solution.py:73
  400.0 352.6 %all-reduce.12.cloned.1.call-start = ((), (), s32[]{:S(2)}) async-start(), calls=%async_computation.4 | async-start | bytes 6291456 | tf_op jit(solution)/shard_map/psum | solution.py:76
  491.0 1.0 copy-start.10
  639.0 6.4 copy-start.15
  643.3 5.6 copy-start.7
  645.9 3.1 copy-start.9
  648.9 0.7 copy-start.13
  656.6 165.3 %all-reduce.14.cloned.1.call-start = ((), (), s32[]{:S(2)}) async-start(), calls=%async_computation.5 | async-start | bytes 2097152 | tf_op jit(solution)/shard_map/psum | solution.py:13
  760.4 315.0 %copy-start.2 = (f32[512,1536]{1,0:T(8,128)}, f32[512,1536]{1,0:T(8,128)S(1)}, u32[]{:S(2)}) copy-start(f32[512,1536]{1,0:T(8,128)S(1)} %convolution_subtract_fusion.1) | copy-start | bytes 9437188
  761.6 151.5 %all-reduce.16.cloned.1.call-start = ((), (), s32[]{:S(2)}) async-start(), calls=%async_computation.6 | async-start | bytes 2097152 | tf_op jit(solution)/shard_map/psum | solution.py:73
  826.4 352.6 %all-reduce.18.cloned.1.call-start = ((), (), s32[]{:S(2)}) async-start(), calls=%async_computation.7 | async-start | bytes 6291456 | tf_op jit(solution)/shard_map/psum | solution.py:76
  917.4 1.0 copy-start.11
  1065.5 6.4 copy-start.16
  1069.8 5.6 copy-start.6
  1072.4 3.1 copy-start.8
  1075.5 0.7 copy-start.12
  1179.0 9.2 copy-start.4
  1179.0 9.2 copy-start.5
  1179.0 10.0 copy-start.1
Sparse Core Ops, SparseCore 0:
  326.6 68.9 all-reduce.7
  400.1 86.5 all-reduce.9
  656.7 95.8 all-reduce.11
  761.7 60.1 all-reduce.13
  826.6 86.5 all-reduce.15
  1083.2 95.7 all-reduce.17
where the time goes:
time: 1210 us; the launch traced here: 1200 us
  waiting for transfers between devices  699 us (58%)
  other arithmetic  312 us (26%)
  local copies, waits for them, and re-layouts  75.2 us (6%)
  matrix products  74.9 us (6%)
  between operations  20.1 us (2%)
  starting transfers between devices  15.3 us (1%)
    all_to_all x1, waiting for transfers between devices, shards(): lax.all_to_all(sent_rows, 'gr', split_axis=0, concat_axis=0, tiled=True)  205 us
    psum x2, waiting for transfers between devices, shards(): coupling = lax.psum(matmul(basis_cols.T, front_work), 'gr')  192 us
    psum x2, waiting for transfers between devices, shards(): gram_one = lax.psum(matmul(panel_block.T, panel_block), 'gr')  173 us
    another operation x30, other arithmetic, shards(): lower_one = jnp.linalg.cholesky(gram_one)  162 us
    psum x2, waiting for transfers between devices, spread(): return lax.psum(kept, axis)  129 us
    another operation x5, other arithmetic, shards(): jax.scipy.linalg.solve_triangular(lower_one, panel_block.T, lower=True)  85.3 us
    dot_general x6, matrix products, matmul(): jnp.dot(left, right, precision=lax.Precision.HIGHEST, preferred_element_t...  39.7 us
    select_n x1, other arithmetic, shards(): limits = jnp.take(stair, own_rows // STAIR_BLOCK)  35.7 us
  transfers between devices with their start and end apart: 8, of which 7 were waited for; matrix products, arithmetic and copies ran while one was open for 7% of the time, Pallas kernels for 0%

commit v1 on v0

--- a/solution.py
+++ b/solution.py
@@ -73,7 +73,9 @@
         gram_one = lax.psum(matmul(panel_block.T, panel_block), "gr")
         lower_one = jnp.linalg.cholesky(gram_one)
         basis_cols = jax.scipy.linalg.solve_triangular(lower_one, panel_block.T, lower=True).T
-        coupling = lax.psum(matmul(basis_cols.T, front_work), "gr")
+        own = matmul(basis_cols.T, front_work)
+        terms = lax.all_gather(own, "gr")
+        coupling = jnp.sum(terms, axis=0)
         front_work = front_work - matmul(basis_cols, coupling)
         blocks.append(coupling)
     stacked = jnp.concatenate(blocks, axis=0)

time: 1210 us -> 1620 us (1.34)
  waiting for transfers between devices: 699 us -> 1070 us
  other arithmetic: 312 us -> 352 us
    all_gather x0 -> x2, waiting for transfers between devices: none -> 567 us  [shards(): terms = lax.all_gather(own, 'gr')]
    psum x2 -> x0, waiting for transfers between devices: 192 us -> none  [shards(): coupling = lax.psum(matmul(basis_cols.T, front_work), 'gr')]
    reduce_sum x0 -> x2, other arithmetic: none -> 41.2 us  [shards(): coupling = jnp.sum(terms, axis=0)]
  transfers between devices with their start and end apart: 8 -> 8, of which waited for: 7 -> 7; matrix products, arithmetic and copies ran while one was open for 7% -> 5% of each run, Pallas kernels for 0% -> 0%
where the time goes in v1:
time: 1620 us; the launch traced here: 1610 us
  waiting for transfers between devices  1070 us (66%)
  other arithmetic  352 us (22%)
  local copies, waits for them, and re-layouts  75.2 us (5%)
  matrix products  74.6 us (5%)
  between operations  20.4 us (1%)
    all_gather x2, waiting for transfers between devices, shards(): terms = lax.all_gather(own, 'gr')  567 us
    all_to_all x1, waiting for transfers between devices, shards(): lax.all_to_all(sent_rows, 'gr', split_axis=0, concat_axis=0, tiled=True)  205 us
    psum x2, waiting for transfers between devices, shards(): gram_one = lax.psum(matmul(panel_block.T, panel_block), 'gr')  173 us
    another operation x30, other arithmetic, shards(): lower_one = jnp.linalg.cholesky(gram_one)  162 us
    psum x2, waiting for transfers between devices, spread(): return lax.psum(kept, axis)  130 us
    another operation x5, other arithmetic, shards(): jax.scipy.linalg.solve_triangular(lower_one, panel_block.T, lower=True)  84.9 us
    reduce_sum x2, other arithmetic, shards(): coupling = jnp.sum(terms, axis=0)  41.2 us
    dot_general x6, matrix products, matmul(): jnp.dot(left, right, precision=lax.Precision.HIGHEST, preferred_element_t...  39.3 us
  transfers between devices with their start and end apart: 8, of which 7 were waited for; matrix products, arithmetic and copies ran while one was open for 5% of the time, Pallas kernels for 0%

profile of v1, /device:TPU:1, one launch (start us, length us, event | category | flops | bytes accessed | tf_op | source)
XLA Modules:
  0.0 1612.2 jit_solution(11178570193207657573)
XLA Ops:
  12.7 7.6 all-to-all-start
  20.3 2.5 scatter_custom_fusion.2
  23.0 10.1 gather_fusion
  33.1 11.6 broadcast_select_fusion
  44.7 6.8 all-to-all-start.1
  54.2 4.4 compare_select_fusion.3
  60.1 35.7 %select_select_fusion.3 = s32[512]{0:T(512)S(1)} fusion(pred[512]{0:T(512)(128)(4,1)S(1)} %get-tuple-element.130, pred[512]{0:T(512)(128)(4,1)S(1)} %get-tuple-element.131, pred[512]{0:T(512)(128)(4,1)S(1)} %get-tuple-element.132, pred[512]{0:T(512)(128)(4,1)S(1)} %get-tuple-element.133, pred[512]{0:T(512)(128)(4,1)S(1)} %get-tuple-element.134, ...), kind=kLoop, calls=%fused_computation.224 | loop fusion | flops 40960 | bytes 33512 | tf_op jit(solution)/shard_map/jit(_take)/select_n | solution.py:66
  96.0 12.3 scatter_custom_fusion.1
  108.4 204.8 %all-to-all-done.1 = f32[16,152,1536]{2,1,0:T(8,128)} async-done(((f32[16,152,1536]{2,1,0:T(8,128)}), f32[16,152,1536]{2,1,0:T(8,128)}, u32[]{:S(2)}, u32[]{:S(2)}) %all-to-all-start.1) | async-done | bytes 14942240 | tf_op jit(solution)/shard_map/all_to_all | solution.py:61
  313.2 9.8 gather_fusion.1
  326.5 69.1 %all-reduce.6.cloned.1.call-done = f32[512,512]{1,0:T(8,128)} async-done(((f32[512,512]{1,0:T(8,128)}), f32[512,512]{1,0:T(8,128)}) %all-reduce.6.cloned.1.call-update) | async-done | bytes 1048592 | tf_op jit(solution)/shard_map/psum | solution.py:13
  395.6 4.4 fusion.88
  400.2 86.4 %all-reduce.8.cloned.1.call-done = f32[512,512]{0,1:T(8,128)} async-done(((f32[512,512]{0,1:T(8,128)}), f32[512,512]{0,1:T(8,128)}) %all-reduce.8.cloned.1.call-update) | async-done | bytes 1048592 | tf_op jit(solution)/shard_map/psum | solution.py:73
  486.6 2.5 copy.11
  492.0 11.7 cholesky.286
  504.8 9.8 custom-call.27
  517.8 11.7 cholesky.305
  531.5 10.2 custom-call.28
  544.1 11.7 cholesky.326
  557.1 9.8 custom-call.29
  569.1 11.7 cholesky.343
  584.7 2.5 select_select_fusion.2
  587.2 11.7 while.4
  598.9 39.9 %custom-call.30 = f32[4,128,128]{1,2,0:T(8,128)} custom-call(f32[4,128,128]{2,1,0:T(8,128)S(1)} %get-tuple-element.18), custom_call_target="InvertDiagBlocksLowerTriangular" | custom-call | tf_op jit(solution)/shard_map/jit(_solve_triangular)/triangular_solve | solution.py:75
  645.8 2.6 convolution_subtract_fusion.7
  649.6 6.9 fusion.13
  656.5 283.5 %all-gather.5.cloned.1.call-done = f32[8192,1536]{1,0:T(8,128)} async-done(((f32[512,1536]{1,0:T(8,128)}), f32[8192,1536]{1,0:T(8,128)}) %all-gather.5.cloned.1.call-update) | async-done | bytes 50331664 | tf_op jit(solution)/shard_map/all_gather | solution.py:77
  940.1 20.4 %reduce_sum.28 = f32[512,1536]{1,0:T(8,128)} reduce(f32[16,512,1536]{2,1,0:T(8,128)} %bitcast.197, f32[]{:T(128)} %constant.211.clone.1), dimensions={0}, to_apply=%region_16.19 | reduce | flops 11796480 | bytes 53477380 | tf_op jit(solution)/shard_map/reduce_sum | solution.py:78
  960.5 7.8 convolution_subtract_fusion.1
  969.6 60.4 %all-reduce.10.cloned.1.call-done = f32[512,512]{1,0:T(8,128)} async-done(((f32[512,512]{1,0:T(8,128)}), f32[512,512]{1,0:T(8,128)}) %all-reduce.10.cloned.1.call-update) | async-done | bytes 1048592 | tf_op jit(solution)/shard_map/psum | solution.py:13
  1030.0 4.4 fusion.89
  1034.9 86.2 %all-reduce.12.cloned.1.call-done = f32[512,512]{0,1:T(8,128)} async-done(((f32[512,512]{0,1:T(8,128)}), f32[512,512]{0,1:T(8,128)}) %all-reduce.12.cloned.1.call-update) | async-done | bytes 1048592 | tf_op jit(solution)/shard_map/psum | solution.py:73
  1121.1 2.5 copy.13
  1126.5 11.7 cholesky.358
  1139.3 9.8 custom-call.31
  1152.3 11.7 cholesky.377
  1166.0 10.0 custom-call.32
  1178.3 11.7 cholesky.398
  1191.3 9.8 custom-call.33
  1203.4 11.7 cholesky.415
  1219.0 2.5 select_select_fusion.1
  1221.5 11.7 while.5
  1233.2 39.9 %custom-call.34 = f32[4,128,128]{1,2,0:T(8,128)} custom-call(f32[4,128,128]{2,1,0:T(8,128)S(1)} %get-tuple-element.19), custom_call_target="InvertDiagBlocksLowerTriangular" | custom-call | tf_op jit(solution)/shard_map/jit(_solve_triangular)/triangular_solve | solution.py:75
  1280.1 2.6 convolution_subtract_fusion.6
  1283.8 6.9 fusion.12
  1290.8 283.6 %all-gather.7.cloned.1.call-done = f32[8192,1536]{1,0:T(8,128)} async-done(((f32[512,1536]{1,0:T(8,128)}), f32[8192,1536]{1,0:T(8,128)}) %all-gather.7.cloned.1.call-update) | async-done | bytes 50331664 | tf_op jit(solution)/shard_map/all_gather | solution.py:77
  1574.3 20.7 %reduce_sum.29 = f32[512,1536]{1,0:T(8,128)} reduce(f32[16,512,1536]{2,1,0:T(8,128)} %bitcast.196, f32[]{:T(128)} %constant.211.clone.1), dimensions={0}, to_apply=%region_19.22 | reduce | flops 11796480 | bytes 53477380 | tf_op jit(solution)/shard_map/reduce_sum | solution.py:78
  1595.1 9.0 convolution_subtract_fusion
  (185 shorter events, 88.1 us)
Async XLA Ops:
  7.2 15.8 copy-start
  12.7 32.0 %all-to-all-start = ((s32[16,1,152]{2,1,0:T(1,128)}), s32[16,1,152]{2,1,0:T(1,128)S(1)}, u32[]{:S(2)}, u32[]{:S(2)}) async-start(s32[16,1,152]{2,1,0:T(1,128)} %all_to_all.9), calls=%async_computation | async-start | bytes 32768 | tf_op jit(solution)/shard_map/all_to_all | solution.py:62
  44.7 8.1 copy-start.14
  44.7 268.5 %all-to-all-start.1 = ((f32[16,152,1536]{2,1,0:T(8,128)}), f32[16,152,1536]{2,1,0:T(8,128)}, u32[]{:S(2)}, u32[]{:S(2)}) async-start(f32[16,152,1536]{2,1,0:T(8,128)} %broadcast_select_fusion), calls=%async_computation.1 | async-start | bytes 29884416 | tf_op jit(solution)/shard_map/all_to_all | solution.py:61
  51.5 344.0 %all-reduce.6.cloned.1.call-start = ((), (), s32[]{:S(2)}) async-start(), calls=%async_computation.2 | async-start | bytes 2097152 | tf_op jit(solution)/shard_map/psum | solution.py:13
  325.3 323.6 %copy-start.3 = (f32[512,1536]{1,0:T(8,128)}, f32[512,1536]{1,0:T(8,128)S(1)}, u32[]{:S(2)}) copy-start(f32[512,1536]{1,0:T(8,128)S(1)} %select_select_fusion) | copy-start | bytes 9437188
  326.5 160.2 %all-reduce.8.cloned.1.call-start = ((), (), s32[]{:S(2)}) async-start(), calls=%async_computation.3 | async-start | bytes 2097152 | tf_op jit(solution)/shard_map/psum | solution.py:73
  400.0 540.1 %all-gather.5.cloned.1.call-start = ((), (), s32[]{:S(2)}) async-start(), calls=%async_computation.6 | async-start | bytes 53477376 | tf_op jit(solution)/shard_map/all_gather | solution.py:77
  490.9 1.0 copy-start.10
  638.9 6.4 copy-start.15
  643.2 5.6 copy-start.7
  645.8 3.1 copy-start.9
  648.9 0.7 copy-start.13
  656.5 373.6 %all-reduce.10.cloned.1.call-start = ((), (), s32[]{:S(2)}) async-start(), calls=%async_computation.4 | async-start | bytes 2097152 | tf_op jit(solution)/shard_map/psum | solution.py:13
  968.3 314.8 %copy-start.2 = (f32[512,1536]{1,0:T(8,128)}, f32[512,1536]{1,0:T(8,128)S(1)}, u32[]{:S(2)}) copy-start(f32[512,1536]{1,0:T(8,128)S(1)} %convolution_subtract_fusion.1) | copy-start | bytes 9437188
  969.5 151.6 %all-reduce.12.cloned.1.call-start = ((), (), s32[]{:S(2)}) async-start(), calls=%async_computation.5 | async-start | bytes 2097152 | tf_op jit(solution)/shard_map/psum | solution.py:73
  1034.4 539.9 %all-gather.7.cloned.1.call-start = ((), (), s32[]{:S(2)}) async-start(), calls=%async_computation.7 | async-start | bytes 53477376 | tf_op jit(solution)/shard_map/all_gather | solution.py:77
  1125.4 1.0 copy-start.11
  1273.2 6.4 copy-start.16
  1277.5 5.6 copy-start.6
  1280.1 3.1 copy-start.8
  1283.1 0.7 copy-start.12
  1595.1 9.0 copy-start.4
  1595.1 9.0 copy-start.5
  1595.1 9.8 copy-start.1
Sparse Core Ops, SparseCore 0:
  326.6 68.9 all-reduce.5
  400.1 86.4 all-reduce.7
  656.6 283.4 all-gather.4
  969.7 60.3 all-reduce.9
  1034.6 86.5 all-reduce.11
  1290.9 283.4 all-gather.6
